TPU v7x, 256 devices: a whole 4x4x8 slice. The times are simulated.
256 devices in a mesh: rows: 64 (over x_lo, y, z), cols: 4 (over x_hi, core).
Axes of the slice: x: 4 (x_hi: 2, x_lo: 2; x = x_hi * 2 + x_lo), y: 4, z: 8, core: 2. Of those that a mesh axis runs over, the one named last changes fastest.
Arguments:
- l_blocks: bfloat16 [2048, 64, 1920], P(('rows', 'cols')), may hold values from -0.25 to 0.25
- s_blocks: bfloat16 [2048, 64, 1280], P('rows', None, 'cols'), may hold values from -6 to 6
- l_index: int32 [2048, 30], P(('rows', 'cols')), may hold values from 0 to 2047, as said below
- s_cols: int32 [2048, 20], replicated, may hold values from 0 to 2047, as said below
- c_index: int32 [2048, 24], P(('rows', 'cols')), may hold values from 0 to 2047, as said below
Outputs:
- product: bfloat16 [2048, 64, 1536], P(('rows', 'cols'))
Inputs may be any that keep to these rules, and one draw needn't show every extreme that they name: `l_index`: the 30 entries of block-row i are distinct and lie in the window of 31 block-rows starting at max(0, min(i - 15, 2017)). `s_cols`: the entries of one block-row are distinct; those in slots p * 5 to (p + 1) * 5 - 1 are congruent to p modulo 20 // 5 and lie within 7 such columns around the block-row. `c_index`: the entries of one block-row are distinct; those in slots p * 6 to (p + 1) * 6 - 1 are congruent to p modulo 24 // 6 and lie within 16 such columns around the block-row.
All inputs are finite; a program needn't handle non-finite values.
Results may differ from a plain program's by a relative error of at most 0.001.
Values may be sent and summed in bfloat16 or wider, within the bound.
No kernel may reach another device: no remote copies, remote signals or barrier semaphores. Data moves between devices by JAX's collectives and lax.ppermute only.
A program may use at most 192 MiB of HBM per device.

v0:
```python
import math
import jax
import jax.numpy as jnp
from jax import lax
from jax.sharding import PartitionSpec as P

HL = 15


def padded(block, sides, width):
    for axis, dim in sides:
        count = lax.axis_size(axis)
        forward = [(i, i + 1) for i in range(count - 1)]
        backward = [(target, source) for source, target in forward]
        low = lax.ppermute(
            lax.slice_in_dim(block, block.shape[dim] - width, None, axis=dim), axis, forward
        )
        high = lax.ppermute(lax.slice_in_dim(block, 0, width, axis=dim), axis, backward)
        block = jnp.concatenate([low, block, high], axis=dim)
    return block


def row_products(l_rows, l_ids, want_index, s_near, slot_cols, first):
    total = l_rows.shape[0]
    width = l_rows.shape[1]
    slot_total = s_near.shape[2] // width
    kept = want_index.shape[1]
    s_four = s_near.reshape(s_near.shape[0], width, slot_total, width)
    s_four = jnp.concatenate(
        [s_four, jnp.zeros((s_four.shape[0], width, 1, width), s_four.dtype)], axis=2
    )
    per_turn = math.gcd(total, max(1, 96 // kept))

    def single(left_row, left_ids, want_cols):
        slot_ids = jnp.take(slot_cols, left_ids, axis=0)
        match = slot_ids[:, None, :] == want_cols[None, :, None]
        slot_pick = jnp.sum(
            jnp.where(match, lax.iota(jnp.int32, slot_total)[None, None, :], 0),
            axis=2,
            dtype=jnp.int32,
        )
        found = jnp.any(match, axis=2)
        slot_pick = jnp.where(found, slot_pick, slot_total)
        local_ids = left_ids - first
        picked = s_four[local_ids[:, None], :, slot_pick, :]
        left_three = left_row.reshape(width, left_ids.shape[0], width)
        summed = jnp.einsum("akb,kmbc->amc", left_three, picked, preferred_element_type=jnp.float32)
        return summed.reshape(width, kept * width).astype(jnp.bfloat16)

    def one_group(group):
        return jax.vmap(single)(group[0], group[1], group[2])

    shaped = tuple(
        (
            a.reshape((total // per_turn, per_turn) + a.shape[1:])
            for a in (l_rows, l_ids, want_index)
        )
    )
    result = lax.map(one_group, shaped)
    return result.reshape((total,) + result.shape[2:])


def shards(l_blocks, s_blocks, l_index, s_cols, c_index):
    row_here = lax.axis_index("rows")
    group_size = s_blocks.shape[0]
    group_first = row_here * group_size
    whole = lax.all_gather(s_blocks, "cols", axis=2, tiled=True)
    nearby = padded(whole, (("rows", 0),), HL)
    return row_products(l_blocks, l_index, c_index, nearby, s_cols, group_first - HL)


def solution(mesh):
    return jax.shard_map(
        shards,
        mesh=mesh,
        in_specs=(
            P(("rows", "cols"), None, None),
            P("rows", None, "cols"),
            P(("rows", "cols"), None),
            P(),
            P(("rows", "cols"), None),
        ),
        out_specs=P(("rows", "cols"), None, None),
        check_vma=False,
    )
```

profile of v0, /device:TPU:2, one launch (start us, length us, event | category | flops | bytes accessed | tf_op | source)
XLA Modules:
  0.0 386.1 jit_solution(16272070342322603991)
XLA Ops:
  6.5 5.9 %copy.44 = bf16[32,64,320]{1,0,2:T(8,128)(2,1)} copy(bf16[32,64,320]{2,1,0:T(8,128)(2,1)} %param.8) | data formatting | bytes 2621440 | tf_op args[1]
  12.5 79.0 %all-gather.2.cloned.1.call-done = bf16[32,64,1280]{1,0,2:T(8,128)(2,1)} async-done(((bf16[32,64,320]{1,0,2:T(8,128)(2,1)}), bf16[32,64,1280]{1,0,2:T(8,128)(2,1)}) %all-gather.2.cloned.1.call-update) | async-done | bytes 5242896 | tf_op jit(solution)/shard_map/all_gather | solution.py:67
  91.4 9.8 %fusion.13 = (bf16[15,64,1280]{1,0,2:T(8,128)(2,1)}, bf16[15,64,1280]{1,0,2:T(8,128)(2,1)}) fusion(bf16[32,64,1280]{1,0,2:T(8,128)(2,1)} %all-gather.2.cloned.1.call-done), kind=kLoop, calls=%fused_computation.26 | loop fusion | bytes 9830400 | tf_op jit(solution)/shard_map/slice | solution.py:16
  101.2 7.1 %copy.45 = bf16[15,64,1280]{2,1,0:T(8,128)(2,1)} copy(bf16[15,64,1280]{1,0,2:T(8,128)(2,1)} %get-tuple-element.104) | data formatting | bytes 4915200 | tf_op jit(solution)/shard_map/slice | solution.py:16
  108.3 3.5 collective-permute-start
  111.8 7.1 %copy.46 = bf16[15,64,1280]{2,1,0:T(8,128)(2,1)} copy(bf16[15,64,1280]{1,0,2:T(8,128)(2,1)} %get-tuple-element.105) | data formatting | bytes 4915200 | tf_op jit(solution)/shard_map/slice | solution.py:18
  118.9 6.9 %collective-permute-start.1 = (bf16[15,64,1280]{2,1,0:T(8,128)(2,1)}, bf16[15,64,1280]{2,1,0:T(8,128)(2,1)}, u32[]{:S(2)}, u32[]{:S(2)}) collective-permute-start(bf16[15,64,1280]{2,1,0:T(8,128)(2,1)} %copy.46), channel_id=1, source_target_pairs={{4,0},{8,4},{12,8},{16,12},{20,16},{24,20},{28,24},{32,28},{36,32}... | collective-permute-start | bytes 7372808 | tf_op jit(solution)/shard_map/ppermute | solution.py:18
  127.2 12.7 %copy.47 = bf16[32,64,1280]{2,1,0:T(8,128)(2,1)} copy(bf16[32,64,1280]{1,0,2:T(8,128)(2,1)} %all-gather.2.cloned.1.call-done) | data formatting | bytes 10485760 | tf_op jit(solution)/shard_map/all_gather | solution.py:67
  139.9 30.7 %collective-permute-done = bf16[15,64,1280]{2,1,0:T(8,128)(2,1)S(1)} collective-permute-done((bf16[15,64,1280]{2,1,0:T(8,128)(2,1)}, bf16[15,64,1280]{2,1,0:T(8,128)(2,1)S(1)}, u32[]{:S(2)}, u32[]{:S(2)}) %collective-permute-start) | collective-permute-done | bytes 2457632 | tf_op jit(solution)/shard_map/ppermute | solution.py:15
  170.6 8.4 %collective-permute-done.1 = bf16[15,64,1280]{2,1,0:T(8,128)(2,1)} collective-permute-done((bf16[15,64,1280]{2,1,0:T(8,128)(2,1)}, bf16[15,64,1280]{2,1,0:T(8,128)(2,1)}, u32[]{:S(2)}, u32[]{:S(2)}) %collective-permute-start.1) | collective-permute-done | bytes 2457632 | tf_op jit(solution)/shard_map/ppermute | solution.py:18
  179.0 8.8 %pad_maximum_fusion = bf16[62,64,1280]{2,1,0:T(8,128)(2,1)} fusion(bf16[15,64,1280]{2,1,0:T(8,128)(2,1)} %collective-permute-done.1, bf16[32,64,1280]{2,1,0:T(8,128)(2,1)} %copy.47, bf16[15,64,1280]{2,1,0:T(8,128)(2,1)S(1)} %collective-permute-done), kind=kLoop, calls=%fused_computation.25 | loop fusion | flops 10158080 | bytes 20316160 | tf_op jit(solution)/shard_map/concatenate | solution.py:19
  187.9 29.2 %reshape.109 = bf16[62,64,20,64]{3,2,1,0:T(8,128)(2,1)} reshape(bf16[62,64,1280]{2,1,0:T(8,128)(2,1)} %pad_maximum_fusion) | data formatting | bytes 20316160 | tf_op jit(solution)/shard_map/reshape | solution.py:28
  217.0 12.8 %copy.54 = bf16[62,64,20,64]{3,1,2,0:T(8,128)(2,1)S(1)} copy(bf16[62,64,20,64]{3,2,1,0:T(8,128)(2,1)} %reshape.109) | data formatting | bytes 20316160
  229.8 11.0 %concatenate.10.clone = bf16[62,64,21,64]{3,1,2,0:T(8,128)(2,1)} pad(bf16[62,64,20,64]{3,1,2,0:T(8,128)(2,1)S(1)} %copy.54, bf16[]{:T(256)} %constant.33.clone.1), padding=0_0x0_0x0_1x0_0 | pad | bytes 20824066 | tf_op jit(solution)/shard_map/concatenate | solution.py:29
  240.8 138.4 %while.10 = (s32[]{:T(128)}, bf16[2,4,64,1536]{3,2,1,0:T(8,128)(2,1)}, bf16[2,4,64,1920]{3,2,1,0:T(8,128)(2,1)}, s32[2,4,30]{2,1,0:T(4,128)S(1)}, s32[]{:T(128)}...) while((s32[]{:T(128)}, ...), condition=%wide.region_3.4_spmd, body=%wide.region_0.3_spmd.sunk | while | flops 1510650240 | bytes 81435040 | solution.py:59
  240.9 1.9 gather_fusion
  243.7 39.2 %gather_fusion.1 = bf16[2880,64,64]{2,1,0:T(8,128)(2,1)} fusion(bf16[62,64,21,64]{3,1,2,0:T(8,128)(2,1)} %get-tuple-element.180, s32[2880]{0:T(1024)S(1)} %reshape.142), kind=kCustom, calls=%fused_computation.1.clone.1 | custom fusion | bytes 47208960 | tf_op jit(solution)/shard_map/while/body/eval_jaxpr/vmap()/gather | solution.py:45
  284.2 2.1 reshape.143
  286.3 19.4 %bitcast_convert_fusion.2 = bf16[4,64,24,64]{3,1,2,0:T(8,128)(2,1)} fusion(bf16[4,30,24,64,64]{4,3,2,1,0:T(8,128)(2,1)} %bitcast.48, bf16[4,64,30,64,1]{3,2,1,0,4:T(8,128)(2,1)S(1)} %bitcast.49), kind=kOutput, calls=%fused_computation.4.clone.1 | convolution fusion | flops 1510342656 | bytes 25362432 | tf_op jit(solution)/shard_map/while/body/eval_jaxpr/vmap(akb,kmbc->amc)/dot_general | solution.py:47
  305.7 2.4 copy.74
  312.9 39.2 %gather_fusion.1 = bf16[2880,64,64]{2,1,0:T(8,128)(2,1)} fusion(bf16[62,64,21,64]{3,1,2,0:T(8,128)(2,1)} %get-tuple-element.180, s32[2880]{0:T(1024)S(1)} %reshape.142), kind=kCustom, calls=%fused_computation.1.clone.1 | custom fusion | bytes 47208960 | tf_op jit(solution)/shard_map/while/body/eval_jaxpr/vmap()/gather | solution.py:45
  353.4 2.1 reshape.143
  355.5 19.4 %bitcast_convert_fusion.2 = bf16[4,64,24,64]{3,1,2,0:T(8,128)(2,1)} fusion(bf16[4,30,24,64,64]{4,3,2,1,0:T(8,128)(2,1)} %bitcast.48, bf16[4,64,30,64,1]{3,2,1,0,4:T(8,128)(2,1)S(1)} %bitcast.49), kind=kOutput, calls=%fused_computation.4.clone.1 | convolution fusion | flops 1510342656 | bytes 25362432 | tf_op jit(solution)/shard_map/while/body/eval_jaxpr/vmap(akb,kmbc->amc)/dot_general | solution.py:47
  374.9 2.4 copy.74
  (47 shorter events, 11.5 us)
Async XLA Ops:
  6.5 84.9 %all-gather.2.cloned.1.call-start = ((), (), s32[]{:S(2)}) async-start(), calls=%async_computation | async-start | bytes 13107200 | tf_op jit(solution)/shard_map/all_gather | solution.py:67
  108.3 62.3 %collective-permute-start = (bf16[15,64,1280]{2,1,0:T(8,128)(2,1)}, bf16[15,64,1280]{2,1,0:T(8,128)(2,1)S(1)}, u32[]{:S(2)}, u32[]{:S(2)}) collective-permute-start(bf16[15,64,1280]{2,1,0:T(8,128)(2,1)} %copy.45), channel_id=1, source_target_pairs={{0,4},{4,8},{8,12},{12,16},{16,20},{20,24},{24,28},{28,32},{32,36}... | collective-permute-start | bytes 7372808 | tf_op jit(solution)/shard_map/ppermute | solution.py:15
  111.8 14.1 %copy-start.1 = (s32[2048,20]{0,1:T(8,128)S(1)}, s32[2048,20]{0,1:T(8,128)}, u32[]{:S(2)}) copy-start(s32[2048,20]{0,1:T(8,128)} %param.10) | copy-start | bytes 491524
  118.9 60.1 %collective-permute-start.1 = (bf16[15,64,1280]{2,1,0:T(8,128)(2,1)}, bf16[15,64,1280]{2,1,0:T(8,128)(2,1)}, u32[]{:S(2)}, u32[]{:S(2)}) collective-permute-start(bf16[15,64,1280]{2,1,0:T(8,128)(2,1)} %copy.46), channel_id=1, source_target_pairs={{4,0},{8,4},{12,8},{16,12},{20,16},{24,20},{28,24},{32,28},{36,32}... | collective-permute-start | bytes 7372808 | tf_op jit(solution)/shard_map/ppermute | solution.py:18
  229.8 11.0 %copy-start = (s32[8,30]{1,0:T(8,128)S(1)}, s32[8,30]{1,0:T(8,128)}, u32[]{:S(2)}) copy-start(s32[8,30]{1,0:T(8,128)} %param.9) | copy-start | bytes 2884
  229.8 11.0 %copy-start.2 = (s32[8,24]{1,0:T(8,128)S(1)}, s32[8,24]{1,0:T(8,128)}, u32[]{:S(2)}) copy-start(s32[8,24]{1,0:T(8,128)} %param.11) | copy-start | bytes 2308
Sparse Core Ops, SparseCore 0:
  12.6 78.8 all-gather.1
where the time goes:
time: 388 us; the launch traced here: 386 us
  local copies, waits for them, and re-layouts  195 us (50%)
  waiting for transfers between devices  118 us (30%)
  matrix products  38.7 us (10%)
  between operations  13.5 us (3%)
  starting transfers between devices  10.4 us (3%)
  other arithmetic  9.79 us (3%)
    all_gather x1, waiting for transfers between devices, shards(): whole = lax.all_gather(s_blocks, 'cols', axis=2, tiled=True)  79 us
    gather x2, local copies, waits for them, and re-layouts, single(): picked = s_four[local_ids[:, None], :, slot_pick, :]  78.4 us
    dot_general x2, matrix products, single(): jnp.einsum('akb,kmbc->amc', left_three, picked, preferred_element_type=jn...  38.7 us
    ppermute x1, waiting for transfers between devices, padded(): lax.ppermute(lax.slice_in_dim(block, block.shape[dim] - width, None, axis...  30.7 us
    reshape x1, local copies, waits for them, and re-layouts, row_products(): s_four = s_near.reshape(s_near.shape[0], width, slot_total, width)  29.2 us
    unnamed x8, local copies, waits for them, and re-layouts  18.7 us
    slice x2, local copies, waits for them, and re-layouts, padded(): lax.slice_in_dim(block, block.shape[dim] - width, None, axis=dim)  16.9 us
    all_gather x1, local copies, waits for them, and re-layouts, shards(): whole = lax.all_gather(s_blocks, 'cols', axis=2, tiled=True)  12.7 us
  transfers between devices with their start and end apart: 3, of which 3 were waited for; matrix products, arithmetic and copies ran while one was open for 5% of the time, Pallas kernels for 0%

commit v1 on v0

--- a/solution.py
+++ b/solution.py
@@ -64,7 +64,8 @@
     row_here = lax.axis_index("rows")
     group_size = s_blocks.shape[0]
     group_first = row_here * group_size
-    whole = lax.all_gather(s_blocks, "cols", axis=2, tiled=True)
+    stack = jnp.stack([s_blocks] * lax.axis_size("cols"))
+    whole = jnp.concatenate(lax.all_to_all(stack, "cols", 0, 0), axis=2)
     nearby = padded(whole, (("rows", 0),), HL)
     return row_products(l_blocks, l_index, c_index, nearby, s_cols, group_first - HL)
 

time: 388 us -> 358 us (0.923)
  waiting for transfers between devices: 118 us -> 13.7 us
  blocking collectives: 0 us -> 75.3 us
  between operations: 13.5 us -> 0.09 us
  other arithmetic: 9.79 us -> 22.8 us
    all_gather x1 -> x0, waiting for transfers between devices: 79 us -> none  [shards(): whole = lax.all_gather(s_blocks, 'cols', axis=2, tiled=True)]
    all_to_all x0 -> x1, blocking collectives: none -> 75.3 us  [shards(): whole = jnp.concatenate(lax.all_to_all(stack, 'cols', 0, 0), axis=2)]
    concatenate x0 -> x3, local copies, waits for them, and re-layouts: none -> 33.8 us  [padded(): block = jnp.concatenate([low, block, high], axis=dim)]
    ppermute x1, waiting for transfers between devices: 30.7 us -> 12.2 us  [padded(): lax.ppermute(lax.slice_in_dim(block, block.shape[dim] - width, None, axis...]
    reshape x1, local copies, waits for them, and re-layouts: 29.2 us -> 11.3 us  [shards(): whole = jnp.concatenate(lax.all_to_all(stack, 'cols', 0, 0), axis=2)]
    concatenate x1, other arithmetic: 8.84 us -> 21.9 us  [padded(): block = jnp.concatenate([low, block, high], axis=dim)]
    all_gather x1 -> x0, local copies, waits for them, and re-layouts: 12.7 us -> none  [shards(): whole = lax.all_gather(s_blocks, 'cols', axis=2, tiled=True)]
    ppermute x1, waiting for transfers between devices: 8.41 us -> 1.52 us  [padded(): lax.ppermute(lax.slice_in_dim(block, 0, width, axis=dim), axis, backward)]
  transfers between devices with their start and end apart: 3 -> 2, of which waited for: 3 -> 2; matrix products, arithmetic and copies ran while one was open for 5% -> 13% of each run, Pallas kernels for 0% -> 0%
where the time goes in v1:
time: 358 us; the launch traced here: 356 us
  local copies, waits for them, and re-layouts  192 us (54%)
  blocking collectives  75.3 us (21%)
  matrix products  38.7 us (11%)
  other arithmetic  22.8 us (6%)
  waiting for transfers between devices  13.7 us (4%)
  starting transfers between devices  13.2 us (4%)
    gather x2, local copies, waits for them, and re-layouts, single(): picked = s_four[local_ids[:, None], :, slot_pick, :]  78.4 us
    all_to_all x1, blocking collectives, shards(): whole = jnp.concatenate(lax.all_to_all(stack, 'cols', 0, 0), axis=2)  75.3 us
    dot_general x2, matrix products, single(): jnp.einsum('akb,kmbc->amc', left_three, picked, preferred_element_type=jn...  38.7 us
    concatenate x3, local copies, waits for them, and re-layouts, padded(): block = jnp.concatenate([low, block, high], axis=dim)  33.8 us
    concatenate x1, other arithmetic, padded(): block = jnp.concatenate([low, block, high], axis=dim)  21.9 us
    unnamed x9, local copies, waits for them, and re-layouts  14.6 us
    ppermute x1, waiting for transfers between devices, padded(): lax.ppermute(lax.slice_in_dim(block, block.shape[dim] - width, None, axis...  12.2 us
    reshape x1, local copies, waits for them, and re-layouts, shards(): whole = jnp.concatenate(lax.all_to_all(stack, 'cols', 0, 0), axis=2)  11.3 us
  transfers between devices with their start and end apart: 2, of which 2 were waited for; matrix products, arithmetic and copies ran while one was open for 13% of the time, Pallas kernels for 0%

profile of v1, /device:TPU:2, one launch (start us, length us, event | category | flops | bytes accessed | tf_op | source)
XLA Modules:
  0.0 356.5 jit_solution(5977913841004731016)
XLA Ops:
  0.0 2.5 stack.2
  2.5 75.3 %all_to_all.5 = bf16[4,32,64,320]{3,2,1,0:T(8,128)(2,1)S(1)} all-to-all(bf16[4,32,64,320]{3,2,1,0:T(8,128)(2,1)S(1)} %stack.2), channel_id=1, replica_groups=mesh['rows'=64,'cols'=4] {'cols'}, dimensions={0} | all-to-all | bytes 10485760 | tf_op jit(solution)/shard_map/all_to_all | solution.py:68
  80.5 4.0 %copy.42 = bf16[15,64,4,320]{3,2,1,0:T(4,128)(2,1)} copy(bf16[15,64,4,320]{3,1,0,2:T(8,128)(2,1)S(1)} %get-tuple-element.104) | data formatting | bytes 4915200 | tf_op jit(solution)/shard_map/slice | solution.py:16
  84.5 5.9 %slice.13 = bf16[15,64,1280]{2,1,0:T(8,128)(2,1)} reshape(bf16[15,64,4,320]{3,2,1,0:T(4,128)(2,1)} %copy.42) | data formatting | bytes 4915200 | tf_op jit(solution)/shard_map/slice | solution.py:16
  90.4 3.8 %collective-permute-start = (bf16[15,64,1280]{2,1,0:T(8,128)(2,1)}, bf16[15,64,1280]{2,1,0:T(8,128)(2,1)}, u32[]{:S(2)}, u32[]{:S(2)}) collective-permute-start(bf16[15,64,1280]{2,1,0:T(8,128)(2,1)} %slice.13), channel_id=1, source_target_pairs={{0,4},{4,8},{8,12},{12,16},{16,20},{20,24},{24,28},{28,32},{32,36}... | collective-permute-start | bytes 7372808 | tf_op jit(solution)/shard_map/ppermute | solution.py:15
  94.2 4.0 %copy.44 = bf16[15,64,4,320]{3,2,1,0:T(4,128)(2,1)} copy(bf16[15,64,4,320]{3,1,0,2:T(8,128)(2,1)S(1)} %get-tuple-element.105) | data formatting | bytes 4915200 | tf_op jit(solution)/shard_map/slice | solution.py:18
  98.2 4.7 %slice.15 = bf16[15,64,1280]{2,1,0:T(8,128)(2,1)S(1)} reshape(bf16[15,64,4,320]{3,2,1,0:T(4,128)(2,1)} %copy.44) | data formatting | bytes 4915200 | tf_op jit(solution)/shard_map/slice | solution.py:18
  103.0 9.4 %collective-permute-start.1 = (bf16[15,64,1280]{2,1,0:T(8,128)(2,1)S(1)}, bf16[15,64,1280]{2,1,0:T(8,128)(2,1)}, u32[]{:S(2)}, u32[]{:S(2)}) collective-permute-start(bf16[15,64,1280]{2,1,0:T(8,128)(2,1)S(1)} %slice.15), channel_id=1, source_target_pairs={{4,0},{8,4},{12,8},{16,12},{20,16},{24,20},{28,24},{32,28},{36,32}... | collective-permute-start | bytes 7372808 | tf_op jit(solution)/shard_map/ppermute | solution.py:18
  113.7 11.3 %copy.43 = bf16[32,64,4,320]{3,2,1,0:T(4,128)(2,1)} copy(bf16[32,64,4,320]{3,1,0,2:T(8,128)(2,1)} %bitcast.51) | data formatting | bytes 10485760 | tf_op jit(solution)/shard_map/reshape | solution.py:68
  125.0 17.6 %concatenate.17 = bf16[32,64,20,64]{3,2,1,0:T(8,128)(2,1)} reshape(bf16[32,64,4,320]{3,2,1,0:T(4,128)(2,1)} %copy.43) | data formatting | bytes 10485760 | tf_op jit(solution)/shard_map/concatenate | solution.py:19
  142.6 12.2 %collective-permute-done = bf16[15,64,1280]{2,1,0:T(8,128)(2,1)} collective-permute-done((bf16[15,64,1280]{2,1,0:T(8,128)(2,1)}, bf16[15,64,1280]{2,1,0:T(8,128)(2,1)}, u32[]{:S(2)}, u32[]{:S(2)}) %collective-permute-start) | collective-permute-done | bytes 2457632 | tf_op jit(solution)/shard_map/ppermute | solution.py:15
  154.8 8.1 %concatenate.16 = bf16[15,64,20,64]{3,2,1,0:T(8,128)(2,1)} reshape(bf16[15,64,1280]{2,1,0:T(8,128)(2,1)} %collective-permute-done) | data formatting | bytes 4915200 | tf_op jit(solution)/shard_map/concatenate | solution.py:19
  164.4 8.1 %concatenate.18 = bf16[15,64,20,64]{3,2,1,0:T(8,128)(2,1)} reshape(bf16[15,64,1280]{2,1,0:T(8,128)(2,1)} %collective-permute-done.1) | data formatting | bytes 4915200 | tf_op jit(solution)/shard_map/concatenate | solution.py:19
  172.5 21.9 %pad_maximum_fusion = bf16[62,64,20,64]{3,2,1,0:T(8,128)(2,1)} fusion(bf16[15,64,20,64]{3,2,1,0:T(8,128)(2,1)} %concatenate.18, bf16[32,64,20,64]{3,2,1,0:T(8,128)(2,1)} %concatenate.17, bf16[15,64,20,64]{3,2,1,0:T(8,128)(2,1)} %concatenate.16), kind=kLoop, calls=%fused_computation.25 | loop fusion | flops 10158080 | bytes 20316160 | tf_op jit(solution)/shard_map/concatenate | solution.py:19
  194.4 12.8 %copy.51 = bf16[62,64,20,64]{3,1,2,0:T(8,128)(2,1)S(1)} copy(bf16[62,64,20,64]{3,2,1,0:T(8,128)(2,1)} %pad_maximum_fusion) | data formatting | bytes 20316160
  207.2 10.9 %concatenate.20.clone = bf16[62,64,21,64]{3,1,2,0:T(8,128)(2,1)} pad(bf16[62,64,20,64]{3,1,2,0:T(8,128)(2,1)S(1)} %copy.51, bf16[]{:T(256)} %constant.33.clone.1), padding=0_0x0_0x0_1x0_0 | pad | bytes 20824066 | tf_op jit(solution)/shard_map/concatenate | solution.py:29
  218.1 138.4 %while.10 = (s32[]{:T(128)}, bf16[2,4,64,1536]{3,2,1,0:T(8,128)(2,1)}, bf16[2,4,64,1920]{3,2,1,0:T(8,128)(2,1)}, s32[2,4,30]{2,1,0:T(4,128)S(1)}, s32[]{:T(128)}...) while((s32[]{:T(128)}, ...), condition=%wide.region_3.4_spmd, body=%wide.region_0.3_spmd.sunk | while | flops 1510650240 | bytes 81435040 | solution.py:59
  221.0 39.2 %gather_fusion.1 = bf16[2880,64,64]{2,1,0:T(8,128)(2,1)} fusion(bf16[62,64,21,64]{3,1,2,0:T(8,128)(2,1)} %get-tuple-element.180, s32[2880]{0:T(1024)S(1)} %reshape.152), kind=kCustom, calls=%fused_computation.1.clone.1 | custom fusion | bytes 47208960 | tf_op jit(solution)/shard_map/while/body/eval_jaxpr/vmap()/gather | solution.py:45
  261.4 2.1 reshape.153
  263.6 19.4 %bitcast_convert_fusion.2 = bf16[4,64,24,64]{3,1,2,0:T(8,128)(2,1)} fusion(bf16[4,30,24,64,64]{4,3,2,1,0:T(8,128)(2,1)} %bitcast.49, bf16[4,64,30,64,1]{3,2,1,0,4:T(8,128)(2,1)S(1)} %bitcast.52), kind=kOutput, calls=%fused_computation.4.clone.1 | convolution fusion | flops 1510342656 | bytes 25362432 | tf_op jit(solution)/shard_map/while/body/eval_jaxpr/vmap(akb,kmbc->amc)/dot_general | solution.py:47
  283.0 2.4 copy.71
  290.2 39.2 %gather_fusion.1 = bf16[2880,64,64]{2,1,0:T(8,128)(2,1)} fusion(bf16[62,64,21,64]{3,1,2,0:T(8,128)(2,1)} %get-tuple-element.180, s32[2880]{0:T(1024)S(1)} %reshape.152), kind=kCustom, calls=%fused_computation.1.clone.1 | custom fusion | bytes 47208960 | tf_op jit(solution)/shard_map/while/body/eval_jaxpr/vmap()/gather | solution.py:45
  332.8 19.4 %bitcast_convert_fusion.2 = bf16[4,64,24,64]{3,1,2,0:T(8,128)(2,1)} fusion(bf16[4,30,24,64,64]{4,3,2,1,0:T(8,128)(2,1)} %bitcast.49, bf16[4,64,30,64,1]{3,2,1,0,4:T(8,128)(2,1)S(1)} %bitcast.52), kind=kOutput, calls=%fused_computation.4.clone.1 | convolution fusion | flops 1510342656 | bytes 25362432 | tf_op jit(solution)/shard_map/while/body/eval_jaxpr/vmap(akb,kmbc->amc)/dot_general | solution.py:47
  352.1 2.4 copy.71
  (51 shorter events, 19.6 us)
Async XLA Ops:
  77.8 2.6 copy-start
  90.4 64.4 %collective-permute-start = (bf16[15,64,1280]{2,1,0:T(8,128)(2,1)}, bf16[15,64,1280]{2,1,0:T(8,128)(2,1)}, u32[]{:S(2)}, u32[]{:S(2)}) collective-permute-start(bf16[15,64,1280]{2,1,0:T(8,128)(2,1)} %slice.13), channel_id=1, source_target_pairs={{0,4},{4,8},{8,12},{12,16},{16,20},{20,24},{24,28},{28,32},{32,36}... | collective-permute-start | bytes 7372808 | tf_op jit(solution)/shard_map/ppermute | solution.py:15
  98.2 14.1 %copy-start.2 = (s32[2048,20]{0,1:T(8,128)S(1)}, s32[2048,20]{0,1:T(8,128)}, u32[]{:S(2)}) copy-start(s32[2048,20]{0,1:T(8,128)} %param.10) | copy-start | bytes 491524
  103.0 61.4 %collective-permute-start.1 = (bf16[15,64,1280]{2,1,0:T(8,128)(2,1)S(1)}, bf16[15,64,1280]{2,1,0:T(8,128)(2,1)}, u32[]{:S(2)}, u32[]{:S(2)}) collective-permute-start(bf16[15,64,1280]{2,1,0:T(8,128)(2,1)S(1)} %slice.15), channel_id=1, source_target_pairs={{4,0},{8,4},{12,8},{16,12},{20,16},{24,20},{28,24},{32,28},{36,32}... | collective-permute-start | bytes 7372808 | tf_op jit(solution)/shard_map/ppermute | solution.py:18
  207.1 10.9 %copy-start.1 = (s32[8,30]{1,0:T(8,128)S(1)}, s32[8,30]{1,0:T(8,128)}, u32[]{:S(2)}) copy-start(s32[8,30]{1,0:T(8,128)} %param.9) | copy-start | bytes 2884
  207.2 10.9 %copy-start.3 = (s32[8,24]{1,0:T(8,128)S(1)}, s32[8,24]{1,0:T(8,128)}, u32[]{:S(2)}) copy-start(s32[8,24]{1,0:T(8,128)} %param.11) | copy-start | bytes 2308
